TPU v7x, 32 devices: a whole 2x2x4 slice. The times are simulated.
32 devices in a mesh: groups: 2 (over x), ctx: 16 (over z, y, core).
Axes of the slice: x: 2, y: 2, z: 4, core: 2. Of those that a mesh axis runs over, the one named last changes fastest.
Arguments:
- hidden: bfloat16 [256, 8192], P('groups', 'ctx'), parts along dimension 0, may hold values from -6 to 6
- attn_gain: bfloat16 [8192], P('ctx'), may hold values from 0.25 to 1.75
- q_weight: bfloat16 [8192, 8192], P(None, 'ctx'), may hold values from -0.0625 to 0.0625
- q_gain: bfloat16 [128], replicated, may hold values from 0.25 to 1.75
- key_cache: bfloat16 [49152, 1024], P(('groups', 'ctx')), parts along dimension 0, may hold values from -64 to 64
- value_cache: bfloat16 [49152, 1024], P(('groups', 'ctx')), parts along dimension 0, may hold values from -6 to 6
- block_limit: int32 [256], P('groups'), parts along dimension 0, may hold values from 0 to 191, as said below
- out_weight: bfloat16 [8192, 8192], P('ctx'), may hold values from -0.09375 to 0.09375
- next_gain: bfloat16 [8192], P('ctx'), may hold values from 0.25 to 1.75
- next_weight: bfloat16 [8192, 8192], P(None, 'ctx'), may hold values from -0.0625 to 0.0625
Outputs:
- new_hidden: bfloat16 [256, 8192], P('groups', 'ctx'), parts along dimension 0
- next_queries: bfloat16 [256, 8192], P('groups', 'ctx'), parts along dimension 0
There are 2 independent parts, one for each index of `groups`. A program takes and returns all parts, laid end to end along the dimension named above; an argument that names none is the same for every part. Nothing has to cross between parts.
Inputs may be any that keep to these rules, and one draw needn't show every extreme that they name: Text token i may attend the visual blocks 0 to block_limit[i], each of 128 visual tokens; some token reaches the last block and some only the first.
All inputs are finite; a program needn't handle non-finite values.
Results may differ from a plain program's by a relative error of at most 0.015.
Values may be sent and summed in bfloat16 or wider, within the bound.
A program may use at most 64 MiB of HBM per device.

v0:
```python
import jax
import jax.numpy as jnp
from jax import lax
from jax.sharding import PartitionSpec as P

BLK = 128
EPSILON = 1e-05


def normalize_project(share, gain_share, weight):
    whole, gains = (
        lax.all_gather(share, "ctx", axis=1, tiled=True),
        lax.all_gather(gain_share, "ctx", axis=0, tiled=True),
    )
    values = whole.astype(jnp.float32)
    factor = lax.rsqrt(jnp.mean(values * values, axis=1, keepdims=True) + EPSILON)
    normed = (values * factor * gains.astype(jnp.float32)).astype(jnp.bfloat16)
    return jnp.dot(normed, weight, preferred_element_type=jnp.float32)


def on_device(
    hidden,
    attn_gain,
    q_weight,
    q_gain,
    key_cache,
    value_cache,
    block_limit,
    out_weight,
    next_gain,
    next_weight,
):
    queries = hidden.shape[0]
    head_dim = q_gain.shape[0]
    devices = lax.axis_size("ctx")
    query = normalize_project(hidden, attn_gain, q_weight)
    heads_here = query.shape[1] // head_dim
    heads_total = heads_here * devices
    kv_heads = key_cache.shape[1] // head_dim
    group_size = heads_total // kv_heads
    shaped = query.reshape(queries, heads_here, head_dim)
    head_mean = jnp.mean(shaped * shaped, axis=-1, keepdims=True)
    query_normed = (shaped * lax.rsqrt(head_mean + EPSILON) * q_gain.astype(jnp.float32)).astype(
        jnp.bfloat16
    )
    local_tokens = key_cache.shape[0]
    device = lax.axis_index("ctx")
    blocks_here = (device * local_tokens + jnp.arange(local_tokens, dtype=jnp.int32)) // BLK
    allowed = blocks_here[None, :] <= block_limit[:, None]
    scale = head_dim ** (-0.5)
    stacked = jnp.swapaxes(query_normed, 0, 1)
    gathered = lax.all_gather(stacked, "ctx", axis=0, tiled=True)
    gathered = gathered.reshape(kv_heads, group_size * queries, head_dim)
    mask = jnp.tile(allowed, (group_size, 1))

    def one_group(group):
        keys = lax.dynamic_slice_in_dim(key_cache, group * head_dim, head_dim, 1)
        values = lax.dynamic_slice_in_dim(value_cache, group * head_dim, head_dim, 1)
        rows = lax.dynamic_index_in_dim(gathered, group, 0, keepdims=False)
        scores = lax.dot_general(
            rows, keys, (((1,), (1,)), ((), ())), preferred_element_type=jnp.float32
        )
        scores = jnp.where(mask, scores * scale, -jnp.inf)
        top = jnp.maximum(jnp.max(scores, axis=1), -1e30)
        expo = jnp.exp(scores - top[:, None])
        sums = jnp.dot(expo.astype(jnp.bfloat16), values, preferred_element_type=jnp.float32)
        return (sums, top, jnp.sum(expo, axis=1))

    sums, top, total = lax.map(one_group, jnp.arange(kv_heads, dtype=jnp.int32))
    decay = jnp.exp(top - lax.pmax(top, "ctx"))
    sums = (sums * decay[:, :, None]).astype(jnp.bfloat16).reshape(heads_total, queries, head_dim)
    total = (total * decay).reshape(heads_total, queries)
    sums = lax.psum_scatter(sums, "ctx", scatter_dimension=0, tiled=True)
    total = lax.psum_scatter(total, "ctx", scatter_dimension=0, tiled=True)
    attended = (sums.astype(jnp.float32) / total[:, :, None]).astype(jnp.bfloat16)
    attended = jnp.swapaxes(attended, 0, 1).reshape(queries, heads_here * head_dim)
    mixed = lax.psum_scatter(
        lax.dot_general(
            out_weight, attended, (((0,), (1,)), ((), ())), preferred_element_type=jnp.float32
        ),
        "ctx",
        scatter_dimension=0,
        tiled=True,
    )
    new_hidden = (hidden.astype(jnp.float32) + mixed.T).astype(jnp.bfloat16)
    next_queries = normalize_project(new_hidden, next_gain, next_weight).astype(jnp.bfloat16)
    return (new_hidden, next_queries)


def solution(mesh):
    in_specs = (
        P("groups", "ctx"),
        P("ctx"),
        P(None, "ctx"),
        P(),
        P(("groups", "ctx"), None),
        P(("groups", "ctx"), None),
        P("groups"),
        P("ctx", None),
        P("ctx"),
        P(None, "ctx"),
    )
    out_specs = (P("groups", "ctx"), P("groups", "ctx"))
    return jax.shard_map(
        on_device, mesh=mesh, in_specs=in_specs, out_specs=out_specs, check_vma=False
    )
```

profile of v0, /device:TPU:0, one launch (start us, length us, event | category | flops | bytes accessed | tf_op | source)
XLA Modules:
  0.0 450.3 jit_solution(18239864491225797498)
XLA Ops:
  8.6 23.2 %all-gather = bf16[16,1,512]{2,1,0:T(2,128)(2,1)S(1)} all-gather(bf16[1,1,512]{2,1,0:T(2,128)(2,1)S(1)} %reshape.113), channel_id=1, replica_groups=mesh['groups'=2,'ctx'=16] {'ctx'}, dimensions={0}, use_global_device_ids=true | all-gather | bytes 17408 | tf_op jit(solution)/shard_map/all_gather | solution.py:13
  32.5 21.4 %all-gather.6.cloned.1.call-done = bf16[128,8192]{1,0:T(8,128)(2,1)} async-done(((bf16[128,512]{1,0:T(8,128)(2,1)}), bf16[128,8192]{1,0:T(8,128)(2,1)}) %all-gather.6.cloned.1.call-update) | async-done | bytes 2097168 | tf_op jit(solution)/shard_map/all_gather | solution.py:12
  56.0 5.3 %fusion.21 = f32[128,512]{1,0:T(8,128)S(1)} fusion(bf16[8192,512]{1,0:T(8,128)(2,1)} %param.14, bf16[128,8192]{1,0:T(8,128)(2,1)} %all-gather.6.cloned.1.call-done, f32[8192]{0:T(1024)S(1)} %bitcast.75, f32[128]{0:T(128)S(1)} %add_rsqrt_fusion.2), kind=kOutput, calls=%fused_computation.29 | convolution fusion | flops 1077936128 | bytes 10781184 | tf_op jit(solution)/shard_map/dot_general | solution.py:18
  62.9 40.4 %all-gather.8.cloned.1.call-done = bf16[64,128,128]{2,1,0:T(8,128)(2,1)} async-done(((bf16[4,128,128]{2,1,0:T(8,128)(2,1)}), bf16[64,128,128]{2,1,0:T(8,128)(2,1)}) %all-gather.8.cloned.1.call-update) | async-done | bytes 2097168 | tf_op jit(solution)/shard_map/all_gather | solution.py:52
  103.3 87.2 %while.15 = (s32[]{:T(128)}, f32[8,1024,128]{2,1,0:T(8,128)}, f32[8,1024]{1,0:T(8,128)S(1)}, f32[8,1024]{1,0:T(8,128)S(1)}, s32[8]{0:T(128)S(1)}, /*index=5*/bf1...) while((s32[]{:T(128)}, f32[8,1024,128]{2,1,0:T(8,128)}, ...), condition=%wide.region_5.6_spmd.clone, body=%wide.region_2.5_spmd.clone.sunk | while | flops 817888256 | bytes 20878068 | solution.py:69
  108.8 2.4 fusion.53
  111.2 2.8 fusion.54
  117.3 2.3 fusion.52
  119.7 2.4 fusion.53
  122.1 2.8 fusion.54
  128.3 2.3 fusion.52
  130.6 2.4 fusion.53
  133.0 2.8 fusion.54
  141.5 2.4 fusion.53
  143.9 2.8 fusion.54
  152.4 2.4 fusion.53
  154.8 2.8 fusion.54
  163.3 2.4 fusion.53
  165.7 2.8 fusion.54
  171.9 2.3 fusion.52
  174.2 2.4 fusion.53
  176.6 2.8 fusion.54
  185.1 2.4 fusion.53
  187.5 2.8 fusion.54
  190.5 59.4 %pmax.7 = f32[8,1024]{1,0:T(8,128)S(1)} all-reduce(f32[8,1024]{1,0:T(8,128)S(1)} %get-tuple-element.52), channel_id=1, replica_groups=mesh['groups'=2,'ctx'=16] {'ctx'}, use_global_device_ids=true, to_apply=%region_6.7 | all-reduce | flops 8192 | bytes 65536 | tf_op jit(solution)/shard_map/pmax | solution.py:70
  249.9 3.9 multiply_convert_fusion
  255.1 57.8 %all-reduce = f32[64,128]{1,0:T(8,128)S(1)} all-reduce(f32[64,128]{1,0:T(8,128)S(1)} %reshape.111), channel_id=3, replica_groups=mesh['groups'=2,'ctx'=16] {'ctx'}, use_global_device_ids=true, to_apply=%region_8.9.clone | all-reduce | flops 8192 | bytes 65536
  314.5 6.6 %convolution_bitcast_fusion.1 = f32[8192,128]{0,1:T(8,128)} fusion(bf16[128,512]{0,1:T(8,128)(2,1)S(1)} %bitcast.73, bf16[512,8192]{1,0:T(8,128)(2,1)} %param.19), kind=kOutput, calls=%fused_computation.16 | convolution fusion | flops 1073741824 | bytes 12713984 | tf_op jit(solution)/shard_map/dot_general | solution.py:78
  321.2 71.8 %reduce-scatter.5.cloned.1.call-done = f32[512,128]{0,1:T(8,128)} async-done(((f32[8192,128]{0,1:T(8,128)}), f32[512,128]{0,1:T(8,128)}) %reduce-scatter.5.cloned.1.call-update) | async-done | bytes 262160 | tf_op jit(solution)/shard_map/reduce_scatter | solution.py:77
  394.6 19.3 %all-gather.1 = bf16[16,1,512]{2,1,0:T(2,128)(2,1)S(1)} all-gather(bf16[1,1,512]{2,1,0:T(2,128)(2,1)S(1)} %reshape.115), channel_id=1, replica_groups=mesh['groups'=2,'ctx'=16] {'ctx'}, dimensions={0}, use_global_device_ids=true | all-gather | bytes 17408 | tf_op jit(solution)/shard_map/all_gather | solution.py:13
  414.0 21.7 %all-gather.10.cloned.1.call-done = bf16[128,8192]{1,0:T(8,128)(2,1)} async-done(((bf16[128,512]{1,0:T(8,128)(2,1)}), bf16[128,8192]{1,0:T(8,128)(2,1)}) %all-gather.10.cloned.1.call-update) | async-done | bytes 2097168 | tf_op jit(solution)/shard_map/all_gather | solution.py:12
  437.8 6.0 %fusion.27 = bf16[128,512]{1,0:T(8,128)(2,1)} fusion(bf16[8192,512]{1,0:T(8,128)(2,1)} %param.21, bf16[128,8192]{1,0:T(8,128)(2,1)} %all-gather.10.cloned.1.call-done, f32[8192]{0:T(1024)S(1)} %bitcast.76, f32[128]{0:T(128)S(1)} %add_rsqrt_fusion.1), kind=kOutput, calls=%fused_computation.34 | convolution fusion | flops 1078001664 | bytes 10650112 | tf_op jit(solution)/shard_map/dot_general | solution.py:18
  (83 shorter events, 29.3 us)
Async XLA Ops:
  7.2 46.8 %all-gather.6.cloned.1.call-start = ((), (), s32[]{:S(2)}) async-start(), calls=%async_computation.2 | async-start | bytes 2228224 | tf_op jit(solution)/shard_map/all_gather | solution.py:12
  7.9 95.4 %all-gather.8.cloned.1.call-start = ((), (), s32[]{:S(2)}) async-start(), calls=%async_computation.3 | async-start | bytes 2228224 | tf_op jit(solution)/shard_map/all_gather | solution.py:52
  56.0 6.7 %copy-start.2 = (s32[128]{0:T(128)S(1)}, s32[128]{0:T(128)}, u32[]{:S(2)}) copy-start(s32[128]{0:T(128)} %param.18) | copy-start | bytes 1540
  62.6 250.7 %reduce-scatter.3.cloned.1.call-start = ((), (), s32[]{:S(2)}) async-start(), calls=%async_computation.4 | async-start | bytes 2228224 | tf_op jit(solution)/shard_map/reduce_scatter | solution.py:73
  249.9 4.0 copy-start.3
  253.8 139.1 %reduce-scatter.5.cloned.1.call-start = ((), (), s32[]{:S(2)}) async-start(), calls=%async_computation.5 | async-start | bytes 4456448 | tf_op jit(solution)/shard_map/reduce_scatter | solution.py:77
  321.1 71.9 %copy-start = (bf16[128,512]{1,0:T(8,128)(2,1)S(1)}, bf16[128,512]{1,0:T(8,128)(2,1)}, u32[]{:S(2)}) copy-start(bf16[128,512]{1,0:T(8,128)(2,1)} %param.12) | copy-start | bytes 393220
  321.1 73.5 %copy-start.1 = (bf16[512]{0:T(512)(128)(2,1)S(1)}, bf16[512]{0:T(512)(128)(2,1)}, u32[]{:S(2)}) copy-start(bf16[512]{0:T(512)(128)(2,1)} %param.20) | copy-start | bytes 3076
  321.1 114.6 %all-gather.10.cloned.1.call-start = ((), (), s32[]{:S(2)}) async-start(), calls=%async_computation.6 | async-start | bytes 2228224 | tf_op jit(solution)/shard_map/all_gather | solution.py:12
Sparse Core Ops, SparseCore 0:
  10.1 43.7 all-gather.5
  62.7 40.5 all-gather.7
  253.9 59.2 reduce-scatter.2
  321.3 71.6 reduce-scatter.4
  395.5 40.1 all-gather.9
where the time goes:
time: 451 us; the launch traced here: 450 us
  blocking collectives  160 us (35%)
  waiting for transfers between devices  156 us (35%)
  matrix products  58.6 us (13%)
  other arithmetic  32 us (7%)
  loops' own time  21.1 us (5%)
  between operations  14.6 us (3%)
  local copies, waits for them, and re-layouts  7.7 us (2%)
    reduce_scatter x1, waiting for transfers between devices, on_device(): lax.psum_scatter(lax.dot_general(out_weight, attended, (((0,), (1,)), (()...  71.8 us
    pmax x1, blocking collectives, on_device(): decay = jnp.exp(top - lax.pmax(top, 'ctx'))  59.4 us
    unnamed x1, blocking collectives  57.8 us
    all_gather x2, waiting for transfers between devices, normalize_project(): lax.all_gather(share, 'ctx', axis=1, tiled=True)  43.1 us
    all_gather x2, blocking collectives, normalize_project(): lax.all_gather(gain_share, 'ctx', axis=0, tiled=True)  42.5 us
    all_gather x1, waiting for transfers between devices, on_device(): gathered = lax.all_gather(stacked, 'ctx', axis=0, tiled=True)  40.4 us
    dot_general x8, matrix products, one_group(): jnp.dot(expo.astype(jnp.bfloat16), values, preferred_element_type=jnp.flo...  22.3 us
    another operation x1, loops' own time, on_device(): sums, top, total = lax.map(one_group, jnp.arange(kv_heads, dtype=jnp.int32))  21.1 us
  transfers between devices with their start and end apart: 5, of which 5 were waited for; matrix products, arithmetic and copies ran while one was open for 0% of the time, Pallas kernels for 0%

commit v1 on v0

--- a/solution.py
+++ b/solution.py
@@ -49,7 +49,16 @@
     allowed = blocks_here[None, :] <= block_limit[:, None]
     scale = head_dim ** (-0.5)
     stacked = jnp.swapaxes(query_normed, 0, 1)
-    gathered = lax.all_gather(stacked, "ctx", axis=0, tiled=True)
+    ways = lax.axis_size("ctx")
+    up = [(d, (d + 1) % ways) for d in range(ways)]
+    down = [(d, (d - 1) % ways) for d in range(ways)]
+    earlier, later = ([stacked], [stacked])
+    for _ in range(ways // 2):
+        earlier.append(lax.ppermute(earlier[-1], "ctx", up))
+    for _ in range((ways - 1) // 2):
+        later.append(lax.ppermute(later[-1], "ctx", down))
+    line = jnp.concatenate([*earlier[::-1], *later[1:]], axis=0)
+    gathered = jnp.roll(line, (lax.axis_index("ctx") - ways // 2) * stacked.shape[0], axis=0)
     gathered = gathered.reshape(kv_heads, group_size * queries, head_dim)
     mask = jnp.tile(allowed, (group_size, 1))
 

time: 451 us -> 485 us (1.075)
  starting transfers between devices: 0.2 us -> 31.4 us
  local copies, waits for them, and re-layouts: 7.7 us -> 27.7 us
  waiting for transfers between devices: 156 us -> 142 us
    all_gather x1 -> x0, waiting for transfers between devices: 40.4 us -> none  [on_device(): gathered = lax.all_gather(stacked, 'ctx', axis=0, tiled=True)]
    ppermute x0 -> x15, starting transfers between devices: none -> 31.2 us  [the longest x7 30.9 us: on_device(): later.append(lax.ppermute(later[-1], 'ctx', down))]
    ppermute x0 -> x15, waiting for transfers between devices: none -> 25.8 us  [the longest x8 25.8 us: on_device(): earlier.append(lax.ppermute(earlier[-1], 'ctx', up))]
    concatenate x0 -> x1, local copies, waits for them, and re-layouts: none -> 16 us  [on_device(): jnp.roll(line, (lax.axis_index('ctx') - ways // 2) * stacked.shape[0], ax...]
  transfers between devices with their start and end apart: 5 -> 19, of which waited for: 5 -> 12; matrix products, arithmetic and copies ran while one was open for 0% -> 0% of each run, Pallas kernels for 0% -> 0%
where the time goes in v1:
time: 485 us; the launch traced here: 484 us
  blocking collectives  158 us (33%)
  waiting for transfers between devices  142 us (29%)
  matrix products  57.9 us (12%)
  starting transfers between devices  31.4 us (6%)
  other arithmetic  31.4 us (6%)
  local copies, waits for them, and re-layouts  27.7 us (6%)
  loops' own time  21.1 us (4%)
  between operations  14.7 us (3%)
    reduce_scatter x1, waiting for transfers between devices, on_device(): lax.psum_scatter(lax.dot_general(out_weight, attended, (((0,), (1,)), (()...  71.8 us
    unnamed x1, blocking collectives  57.9 us
    pmax x1, blocking collectives, on_device(): decay = jnp.exp(top - lax.pmax(top, 'ctx'))  57.6 us
    all_gather x2, waiting for transfers between devices, normalize_project(): lax.all_gather(share, 'ctx', axis=1, tiled=True)  43 us
    all_gather x2, blocking collectives, normalize_project(): lax.all_gather(gain_share, 'ctx', axis=0, tiled=True)  42.5 us
    ppermute x7, starting transfers between devices, on_device(): later.append(lax.ppermute(later[-1], 'ctx', down))  30.9 us
    ppermute x8, waiting for transfers between devices, on_device(): earlier.append(lax.ppermute(earlier[-1], 'ctx', up))  25.8 us
    dot_general x8, matrix products, one_group(): jnp.dot(expo.astype(jnp.bfloat16), values, preferred_element_type=jnp.flo...  22.3 us
  transfers between devices with their start and end apart: 19, of which 12 were waited for; matrix products, arithmetic and copies ran while one was open for 0% of the time, Pallas kernels for 0%

profile of v1, /device:TPU:0, one launch (start us, length us, event | category | flops | bytes accessed | tf_op | source)
XLA Modules:
  0.0 483.8 jit_solution(8343925461991258239)
XLA Ops:
  8.6 23.2 %all-gather = bf16[16,1,512]{2,1,0:T(2,128)(2,1)S(1)} all-gather(bf16[1,1,512]{2,1,0:T(2,128)(2,1)S(1)} %reshape.113), channel_id=1, replica_groups=mesh['groups'=2,'ctx'=16] {'ctx'}, dimensions={0}, use_global_device_ids=true | all-gather | bytes 17408 | tf_op jit(solution)/shard_map/all_gather | solution.py:13
  32.5 21.4 %all-gather.5.cloned.1.call-done = bf16[128,8192]{1,0:T(8,128)(2,1)} async-done(((bf16[128,512]{1,0:T(8,128)(2,1)}), bf16[128,8192]{1,0:T(8,128)(2,1)}) %all-gather.5.cloned.1.call-update) | async-done | bytes 2097168 | tf_op jit(solution)/shard_map/all_gather | solution.py:12
  56.0 5.3 %fusion.21 = f32[128,512]{1,0:T(8,128)S(1)} fusion(bf16[8192,512]{1,0:T(8,128)(2,1)} %param.14, bf16[128,8192]{1,0:T(8,128)(2,1)} %all-gather.5.cloned.1.call-done, f32[8192]{0:T(1024)S(1)} %bitcast.64, f32[128]{0:T(128)S(1)} %add_rsqrt_fusion.2), kind=kOutput, calls=%fused_computation.29 | convolution fusion | flops 1077936128 | bytes 10781184 | tf_op jit(solution)/shard_map/dot_general | solution.py:18
  62.2 4.2 collective-permute-start.8
  69.1 4.5 collective-permute-start.9
  76.3 4.4 collective-permute-start.10
  80.7 2.7 collective-permute-done.2
  83.5 4.4 collective-permute-start.11
  87.9 2.7 collective-permute-done.3
  90.7 4.4 collective-permute-start.12
  97.9 4.4 collective-permute-start.13
  102.3 2.7 collective-permute-done.5
  105.1 4.5 collective-permute-start.14
  112.4 6.8 %collective-permute-done.7 = bf16[4,128,128]{2,0,1:T(4,128)(2,1)S(1)} collective-permute-done((bf16[4,128,128]{2,0,1:T(4,128)(2,1)S(1)}, bf16[4,128,128]{2,0,1:T(4,128)(2,1)S(1)}, u32[]{:S(2)}, u32[]{:S(2)}) %collective-permute-start.7) | collective-permute-done | bytes 131104 | tf_op jit(solution)/shard_map/ppermute | solution.py:57
  119.2 16.0 %concatenate.6 = bf16[128,128,128]{2,0,1:T(8,128)(2,1)} concatenate(bf16[4,128,128]{2,0,1:T(4,128)(2,1)S(1)} %collective-permute-done.7, bf16[4,128,128]{2,0,1:T(4,128)(2,1)S(1)} %collective-permute-done.6, bf16[4,128,128]{2,0,1:T(4,128)(2,1)S(1)} %collective-permute-done.5, bf16[4,128,128]{2,0,1:T(4,128)(2,1)S(1)} %collective-permute-done.4, ...), dimensions={0} | concatenate | bytes 8388608 | tf_op jit(solution)/shard_map/jit(_roll_dynamic)/concatenate | solution.py:61
  139.3 86.5 %while.15 = (s32[]{:T(128)}, f32[8,1024,128]{2,1,0:T(8,128)}, f32[8,1024]{1,0:T(8,128)S(1)}, f32[8,1024]{1,0:T(8,128)S(1)}, s32[8]{0:T(128)S(1)}, /*index=5*/bf1...) while((s32[]{:T(128)}, f32[8,1024,128]{2,1,0:T(8,128)}, ...), condition=%wide.region_5.6_spmd.clone, body=%wide.region_2.5_spmd.clone.sunk | while | flops 817888256 | bytes 20878068 | solution.py:78
  147.2 2.8 fusion.51
  158.0 2.8 fusion.51
  168.8 2.8 fusion.51
  179.6 2.8 fusion.51
  190.4 2.8 fusion.51
  201.2 2.8 fusion.51
  212.1 2.8 fusion.51
  222.9 2.8 fusion.51
  225.9 57.6 %pmax.7 = f32[8,1024]{1,0:T(8,128)S(1)} all-reduce(f32[8,1024]{1,0:T(8,128)S(1)} %get-tuple-element.52), channel_id=1, replica_groups=mesh['groups'=2,'ctx'=16] {'ctx'}, use_global_device_ids=true, to_apply=%region_6.7 | all-reduce | flops 8192 | bytes 65536 | tf_op jit(solution)/shard_map/pmax | solution.py:79
  283.5 3.8 multiply_convert_fusion
  288.7 57.9 %all-reduce = f32[64,128]{1,0:T(8,128)S(1)} all-reduce(f32[64,128]{1,0:T(8,128)S(1)} %reshape.111), channel_id=3, replica_groups=mesh['groups'=2,'ctx'=16] {'ctx'}, use_global_device_ids=true, to_apply=%region_8.9.clone | all-reduce | flops 8192 | bytes 65536
  348.1 6.6 %convolution_bitcast_fusion.1 = f32[8192,128]{0,1:T(8,128)} fusion(bf16[128,512]{0,1:T(8,128)(2,1)S(1)} %bitcast.62, bf16[512,8192]{1,0:T(8,128)(2,1)} %param.19), kind=kOutput, calls=%fused_computation.16 | convolution fusion | flops 1073741824 | bytes 12713984 | tf_op jit(solution)/shard_map/dot_general | solution.py:87
  354.8 71.8 %reduce-scatter.5.cloned.1.call-done = f32[512,128]{0,1:T(8,128)} async-done(((f32[8192,128]{0,1:T(8,128)}), f32[512,128]{0,1:T(8,128)}) %reduce-scatter.5.cloned.1.call-update) | async-done | bytes 262160 | tf_op jit(solution)/shard_map/reduce_scatter | solution.py:86
  428.3 19.3 %all-gather.1 = bf16[16,1,512]{2,1,0:T(2,128)(2,1)S(1)} all-gather(bf16[1,1,512]{2,1,0:T(2,128)(2,1)S(1)} %reshape.115), channel_id=1, replica_groups=mesh['groups'=2,'ctx'=16] {'ctx'}, dimensions={0}, use_global_device_ids=true | all-gather | bytes 17408 | tf_op jit(solution)/shard_map/all_gather | solution.py:13
  447.6 21.6 %all-gather.7.cloned.1.call-done = bf16[128,8192]{1,0:T(8,128)(2,1)} async-done(((bf16[128,512]{1,0:T(8,128)(2,1)}), bf16[128,8192]{1,0:T(8,128)(2,1)}) %all-gather.7.cloned.1.call-update) | async-done | bytes 2097168 | tf_op jit(solution)/shard_map/all_gather | solution.py:12
  471.3 6.0 %fusion.27 = bf16[128,512]{1,0:T(8,128)(2,1)} fusion(bf16[8192,512]{1,0:T(8,128)(2,1)} %param.21, bf16[128,8192]{1,0:T(8,128)(2,1)} %all-gather.7.cloned.1.call-done, f32[8192]{0:T(1024)S(1)} %bitcast.65, f32[128]{0:T(128)S(1)} %add_rsqrt_fusion.1), kind=kOutput, calls=%fused_computation.34 | convolution fusion | flops 1078001664 | bytes 10650112 | tf_op jit(solution)/shard_map/dot_general | solution.py:18
  (112 shorter events, 69.3 us)
Async XLA Ops:
  7.2 46.8 %all-gather.5.cloned.1.call-start = ((), (), s32[]{:S(2)}) async-start(), calls=%async_computation.2 | async-start | bytes 2228224 | tf_op jit(solution)/shard_map/all_gather | solution.py:12
  7.9 339.0 %reduce-scatter.3.cloned.1.call-start = ((), (), s32[]{:S(2)}) async-start(), calls=%async_computation.3 | async-start | bytes 2228224 | tf_op jit(solution)/shard_map/reduce_scatter | solution.py:82
  56.0 56.1 %copy-start.2 = (s32[128]{0:T(128)S(1)}, s32[128]{0:T(128)}, u32[]{:S(2)}) copy-start(s32[128]{0:T(128)} %param.18) | copy-start | bytes 1540
  61.9 7.2 %collective-permute-start = (bf16[4,128,128]{2,0,1:T(4,128)(2,1)S(1)}, bf16[4,128,128]{2,0,1:T(4,128)(2,1)S(1)}, u32[]{:S(2)}, u32[]{:S(2)}) collective-permute-start(bf16[4,128,128]{2,0,1:T(4,128)(2,1)S(1)} %fusion.31), channel_id=1, source_target_pairs={{0,1},{1,2},{2,3},{3,4},{4,5},{5,6},{6,7},{7,8},{8,9},{9,10},{10,1... | collective-permute-start | bytes 393224 | tf_op jit(solution)/shard_map/ppermute | solution.py:57
  62.2 6.9 %collective-permute-start.8 = (bf16[4,128,128]{2,0,1:T(4,128)(2,1)S(1)}, bf16[4,128,128]{2,0,1:T(4,128)(2,1)S(1)}, u32[]{:S(2)}, u32[]{:S(2)}) collective-permute-start(bf16[4,128,128]{2,0,1:T(4,128)(2,1)S(1)} %fusion.31), channel_id=1, source_target_pairs={{0,15},{1,0},{2,1},{3,2},{4,3},{5,4},{6,5},{7,6},{8,7},{9,8},{10,9... | collective-permute-start | bytes 393224 | tf_op jit(solution)/shard_map/ppermute | solution.py:59
  69.1 7.2 %collective-permute-start.1 = (bf16[4,128,128]{2,0,1:T(4,128)(2,1)S(1)}, bf16[4,128,128]{2,0,1:T(4,128)(2,1)S(1)}, u32[]{:S(2)}, u32[]{:S(2)}) collective-permute-start(bf16[4,128,128]{2,0,1:T(4,128)(2,1)S(1)} %collective-permute-done), channel_id=1, source_target_pairs={{0,1},{1,2},{2,3},{3,4},{4,5},{5,6},{6,7},{7,8},{8,9},{9,10},{10,1... | collective-permute-start | bytes 393224 | tf_op jit(solution)/shard_map/ppermute | solution.py:57
  69.1 7.2 %collective-permute-start.9 = (bf16[4,128,128]{2,0,1:T(4,128)(2,1)S(1)}, bf16[4,128,128]{2,0,1:T(4,128)(2,1)S(1)}, u32[]{:S(2)}, u32[]{:S(2)}) collective-permute-start(bf16[4,128,128]{2,0,1:T(4,128)(2,1)S(1)} %collective-permute-done.8), channel_id=1, source_target_pairs={{0,15},{1,0},{2,1},{3,2},{4,3},{5,4},{6,5},{7,6},{8,7},{9,8},{10,9... | collective-permute-start | bytes 393224 | tf_op jit(solution)/shard_map/ppermute | solution.py:59
  76.3 7.2 %collective-permute-start.2 = (bf16[4,128,128]{2,0,1:T(4,128)(2,1)S(1)}, bf16[4,128,128]{2,0,1:T(4,128)(2,1)S(1)}, u32[]{:S(2)}, u32[]{:S(2)}) collective-permute-start(bf16[4,128,128]{2,0,1:T(4,128)(2,1)S(1)} %collective-permute-done.1), channel_id=1, source_target_pairs={{0,1},{1,2},{2,3},{3,4},{4,5},{5,6},{6,7},{7,8},{8,9},{9,10},{10,1... | collective-permute-start | bytes 393224 | tf_op jit(solution)/shard_map/ppermute | solution.py:57
  76.3 7.2 %collective-permute-start.10 = (bf16[4,128,128]{2,0,1:T(4,128)(2,1)S(1)}, bf16[4,128,128]{2,0,1:T(4,128)(2,1)S(1)}, u32[]{:S(2)}, u32[]{:S(2)}) collective-permute-start(bf16[4,128,128]{2,0,1:T(4,128)(2,1)S(1)} %collective-permute-done.9), channel_id=1, source_target_pairs={{0,15},{1,0},{2,1},{3,2},{4,3},{5,4},{6,5},{7,6},{8,7},{9,8},{10,9... | collective-permute-start | bytes 393224 | tf_op jit(solution)/shard_map/ppermute | solution.py:59
  83.5 7.2 %collective-permute-start.3 = (bf16[4,128,128]{2,0,1:T(4,128)(2,1)S(1)}, bf16[4,128,128]{2,0,1:T(4,128)(2,1)S(1)}, u32[]{:S(2)}, u32[]{:S(2)}) collective-permute-start(bf16[4,128,128]{2,0,1:T(4,128)(2,1)S(1)} %collective-permute-done.2), channel_id=1, source_target_pairs={{0,1},{1,2},{2,3},{3,4},{4,5},{5,6},{6,7},{7,8},{8,9},{9,10},{10,1... | collective-permute-start | bytes 393224 | tf_op jit(solution)/shard_map/ppermute | solution.py:57
  83.5 7.2 %collective-permute-start.11 = (bf16[4,128,128]{2,0,1:T(4,128)(2,1)S(1)}, bf16[4,128,128]{2,0,1:T(4,128)(2,1)S(1)}, u32[]{:S(2)}, u32[]{:S(2)}) collective-permute-start(bf16[4,128,128]{2,0,1:T(4,128)(2,1)S(1)} %collective-permute-done.10), channel_id=1, source_target_pairs={{0,15},{1,0},{2,1},{3,2},{4,3},{5,4},{6,5},{7,6},{8,7},{9,8},{10,9... | collective-permute-start | bytes 393224 | tf_op jit(solution)/shard_map/ppermute | solution.py:59
  90.7 7.2 %collective-permute-start.4 = (bf16[4,128,128]{2,0,1:T(4,128)(2,1)S(1)}, bf16[4,128,128]{2,0,1:T(4,128)(2,1)S(1)}, u32[]{:S(2)}, u32[]{:S(2)}) collective-permute-start(bf16[4,128,128]{2,0,1:T(4,128)(2,1)S(1)} %collective-permute-done.3), channel_id=1, source_target_pairs={{0,1},{1,2},{2,3},{3,4},{4,5},{5,6},{6,7},{7,8},{8,9},{9,10},{10,1... | collective-permute-start | bytes 393224 | tf_op jit(solution)/shard_map/ppermute | solution.py:57
  90.7 7.2 %collective-permute-start.12 = (bf16[4,128,128]{2,0,1:T(4,128)(2,1)S(1)}, bf16[4,128,128]{2,0,1:T(4,128)(2,1)S(1)}, u32[]{:S(2)}, u32[]{:S(2)}) collective-permute-start(bf16[4,128,128]{2,0,1:T(4,128)(2,1)S(1)} %collective-permute-done.11), channel_id=1, source_target_pairs={{0,15},{1,0},{2,1},{3,2},{4,3},{5,4},{6,5},{7,6},{8,7},{9,8},{10,9... | collective-permute-start | bytes 393224 | tf_op jit(solution)/shard_map/ppermute | solution.py:59
  97.9 7.2 %collective-permute-start.5 = (bf16[4,128,128]{2,0,1:T(4,128)(2,1)S(1)}, bf16[4,128,128]{2,0,1:T(4,128)(2,1)S(1)}, u32[]{:S(2)}, u32[]{:S(2)}) collective-permute-start(bf16[4,128,128]{2,0,1:T(4,128)(2,1)S(1)} %collective-permute-done.4), channel_id=1, source_target_pairs={{0,1},{1,2},{2,3},{3,4},{4,5},{5,6},{6,7},{7,8},{8,9},{9,10},{10,1... | collective-permute-start | bytes 393224 | tf_op jit(solution)/shard_map/ppermute | solution.py:57
  97.9 7.2 %collective-permute-start.13 = (bf16[4,128,128]{2,0,1:T(4,128)(2,1)S(1)}, bf16[4,128,128]{2,0,1:T(4,128)(2,1)S(1)}, u32[]{:S(2)}, u32[]{:S(2)}) collective-permute-start(bf16[4,128,128]{2,0,1:T(4,128)(2,1)S(1)} %collective-permute-done.12), channel_id=1, source_target_pairs={{0,15},{1,0},{2,1},{3,2},{4,3},{5,4},{6,5},{7,6},{8,7},{9,8},{10,9... | collective-permute-start | bytes 393224 | tf_op jit(solution)/shard_map/ppermute | solution.py:59
  105.0 7.1 %collective-permute-start.6 = (bf16[4,128,128]{2,0,1:T(4,128)(2,1)S(1)}, bf16[4,128,128]{2,0,1:T(4,128)(2,1)S(1)}, u32[]{:S(2)}, u32[]{:S(2)}) collective-permute-start(bf16[4,128,128]{2,0,1:T(4,128)(2,1)S(1)} %collective-permute-done.5), channel_id=1, source_target_pairs={{0,1},{1,2},{2,3},{3,4},{4,5},{5,6},{6,7},{7,8},{8,9},{9,10},{10,1... | collective-permute-start | bytes 393224 | tf_op jit(solution)/shard_map/ppermute | solution.py:57
  105.1 7.3 %collective-permute-start.14 = (bf16[4,128,128]{2,0,1:T(4,128)(2,1)S(1)}, bf16[4,128,128]{2,0,1:T(4,128)(2,1)S(1)}, u32[]{:S(2)}, u32[]{:S(2)}) collective-permute-start(bf16[4,128,128]{2,0,1:T(4,128)(2,1)S(1)} %collective-permute-done.13), channel_id=1, source_target_pairs={{0,15},{1,0},{2,1},{3,2},{4,3},{5,4},{6,5},{7,6},{8,7},{9,8},{10,9... | collective-permute-start | bytes 393224 | tf_op jit(solution)/shard_map/ppermute | solution.py:59
  112.1 7.1 %collective-permute-start.7 = (bf16[4,128,128]{2,0,1:T(4,128)(2,1)S(1)}, bf16[4,128,128]{2,0,1:T(4,128)(2,1)S(1)}, u32[]{:S(2)}, u32[]{:S(2)}) collective-permute-start(bf16[4,128,128]{2,0,1:T(4,128)(2,1)S(1)} %collective-permute-done.6), channel_id=1, source_target_pairs={{0,1},{1,2},{2,3},{3,4},{4,5},{5,6},{6,7},{7,8},{8,9},{9,10},{10,1... | collective-permute-start | bytes 393224 | tf_op jit(solution)/shard_map/ppermute | solution.py:57
  283.5 3.9 copy-start.3
  287.4 139.3 %reduce-scatter.5.cloned.1.call-start = ((), (), s32[]{:S(2)}) async-start(), calls=%async_computation.4 | async-start | bytes 4456448 | tf_op jit(solution)/shard_map/reduce_scatter | solution.py:86
  354.8 71.9 %copy-start = (bf16[128,512]{1,0:T(8,128)(2,1)S(1)}, bf16[128,512]{1,0:T(8,128)(2,1)}, u32[]{:S(2)}) copy-start(bf16[128,512]{1,0:T(8,128)(2,1)} %param.12) | copy-start | bytes 393220
  354.8 73.5 %copy-start.1 = (bf16[512]{0:T(512)(128)(2,1)S(1)}, bf16[512]{0:T(512)(128)(2,1)}, u32[]{:S(2)}) copy-start(bf16[512]{0:T(512)(128)(2,1)} %param.20) | copy-start | bytes 3076
  354.8 114.4 %all-gather.7.cloned.1.call-start = ((), (), s32[]{:S(2)}) async-start(), calls=%async_computation.5 | async-start | bytes 2228224 | tf_op jit(solution)/shard_map/all_gather | solution.py:12
Sparse Core Ops, SparseCore 0:
  10.1 43.7 all-gather.4
  287.5 59.3 reduce-scatter.2
  354.9 71.6 reduce-scatter.4
  429.2 39.9 all-gather.6
